TPU v7x, 32 devices: a whole 2x2x4 slice. The times are simulated.
32 devices in a mesh: snap: 2 (over core), brick: 16 (over z, y, x).
Axes of the slice: x: 2, y: 2, z: 4, core: 2. Of those that a mesh axis runs over, the one named last changes fastest.
Arguments:
- atom_features: bfloat16 [2, 32, 262144], P('snap', None, 'brick'), may hold values from -6 to 6
- cotangent: bfloat16 [2, 32, 262144], P('snap', None, 'brick'), may hold values from -6 to 6
- cell_index: int32 [2, 4, 262144], P('snap', None, 'brick'), may hold values from 0 to 39, as said below
- assign_weight: float32 [2, 4, 262144], P('snap', None, 'brick'), may hold values from 0.05 to 1
- conv_kernel: bfloat16 [27, 32, 32], replicated, may hold values from -0.21875 to 0.21875
- spectral_gain: float32 [32, 128, 128], P(None, None, 'brick'), may hold values from 0.1 to 2
Outputs:
- atom_grad: bfloat16 [2, 32, 262144], P('snap', None, 'brick')
- kernel_grad: float32 [27, 32, 32], replicated
- gain_grad: float32 [32, 128, 128], P(None, None, 'brick')
Inputs may be any that keep to these rules, and one draw needn't show every extreme that they name: `cell_index`: for each slot there are p from 0 to 8 and z from 0 to 2 such that its four corners are, in order, p * 4 + z, (p + 1) * 4 + z, p * 4 + z + 1 and (p + 1) * 4 + z + 1.
All inputs are finite; a program needn't handle non-finite values.
Results may differ from a plain program's by a relative error of at most 0.0058.
Values may be sent and summed in bfloat16 or wider, within the bound.
A program may use at most 64 MiB of HBM per device.

v0:
```python
import math

import jax
import jax.numpy as jnp
from jax import lax
import numpy as np
from jax.experimental import pallas as pl
from jax.experimental.pallas import tpu as pltpu
from jax.sharding import PartitionSpec as P

NX = 128
NY = 128
NZ = 4
CORNERS = 4


HIGHEST = lax.Precision.HIGHEST


def from_behind(value, axis, steps):
    count = lax.axis_size(axis)
    pairs = [(source, (source + steps) % count) for source in range(count)]
    return lax.ppermute(value, axis, pairs)


def with_halo(cells, sides, width):
    for axis, dim in sides:
        count = lax.axis_size(axis)
        head = lax.slice_in_dim(cells, 0, width, axis=dim)
        tail = lax.slice_in_dim(cells, cells.shape[dim] - width, cells.shape[dim], axis=dim)
        cells = jnp.concatenate(
            [
                lax.ppermute(tail, axis, [(i, (i + 1) % count) for i in range(count)]),
                cells,
                lax.ppermute(head, axis, [((i + 1) % count, i) for i in range(count)]),
            ],
            axis=dim,
        )
    return cells


def tables(length):
    indices = jnp.arange(length, dtype=jnp.int32)
    phases = indices[:, None] * indices[None, :] % length
    angles = phases.astype(jnp.float32) * (2.0 * math.pi / length)
    return (jnp.cos(angles), jnp.sin(angles))


def patches(padded, first_plane, planes):
    row_total = padded.shape[1]
    thickness = padded.shape[3]
    wrapped = jnp.concatenate([padded[:, -1:], padded, padded[:, :1]], axis=1)
    widened = jnp.pad(wrapped, ((0, 0), (0, 0), (0, 0), (1, 1)))
    pieces = []
    for step_first in (-1, 0, 1):
        for step_second in (-1, 0, 1):
            for step_third in (-1, 0, 1):
                pieces.append(
                    widened[
                        :,
                        1 + step_second : 1 + step_second + row_total,
                        first_plane + step_first : first_plane + step_first + planes,
                        1 + step_third : 1 + step_third + thickness,
                    ]
                )
    return jnp.stack(pieces)


def transform_rows(mesh_field, row_cosine, row_sine):
    real_part = jnp.einsum("cyxz,yk->ckxz", mesh_field, row_cosine, precision=HIGHEST)
    imag_part = -jnp.einsum("cyxz,yk->ckxz", mesh_field, row_sine, precision=HIGHEST)
    return jnp.stack([real_part, imag_part])


def transform_columns(stacked, col_cosine, col_sine, sign_value):

    def apply_table(part_values, table):
        return jnp.einsum("ckxz,xq->ckqz", part_values, table, precision=HIGHEST)

    real_part = stacked[0]
    imag_part = stacked[1]
    new_real = apply_table(real_part, col_cosine) + sign_value * apply_table(imag_part, col_sine)
    new_imag = apply_table(imag_part, col_cosine) - sign_value * apply_table(real_part, col_sine)
    return jnp.stack([new_real, new_imag])


def shards(atom_features, cotangent, cell_index, assign_weight, conv_kernel, spectral_gain):
    channels = atom_features.shape[1]
    slot_count = atom_features.shape[2] // NY
    own_planes = NX // lax.axis_size("brick")
    tile_cells = (own_planes + 2) * NZ
    snap_count = lax.axis_size("snap")
    index_tiles = cell_index[0].reshape(CORNERS, NY, slot_count)
    weight_tiles = assign_weight[0].astype(jnp.bfloat16).reshape(CORNERS, NY, slot_count)
    cell_numbers = jnp.arange(tile_cells, dtype=jnp.int32)
    blocks = jnp.zeros((NY, tile_cells, slot_count), jnp.bfloat16)
    for corner in range(CORNERS):
        matches = index_tiles[corner][:, None, :] == cell_numbers[None, :, None]
        blocks = blocks + jnp.where(
            matches, weight_tiles[corner][:, None, :], jnp.zeros((), jnp.bfloat16)
        )
    stacked = jnp.concatenate([atom_features[0], cotangent[0]], axis=0).reshape(
        2 * channels, NY, slot_count
    )
    spread = jnp.einsum("cts,tjs->ctj", stacked, blocks, preferred_element_type=jnp.float32)
    spread = spread.reshape(2 * channels, NY, own_planes + 2, NZ)
    from_above = from_behind(spread[:, :, 0], "brick", -1)
    from_below = from_behind(spread[:, :, own_planes + 1], "brick", 1)
    owned_planes = spread[:, :, 1 : own_planes + 1]
    owned_planes = owned_planes.at[:, :, 0].add(from_below)
    owned_planes = owned_planes.at[:, :, own_planes - 1].add(from_above)
    state_bf = owned_planes[:channels].astype(jnp.bfloat16)
    grad_mesh = owned_planes[channels:]
    col_cosine, col_sine = tables(NX)
    row_cosine, row_sine = tables(NY)

    def make_rows(mesh_field):
        return transform_rows(mesh_field, row_cosine, row_sine)

    def to_columns(part_rows):
        return transform_columns(part_rows, col_cosine, col_sine, 1.0)

    grad_rows = make_rows(grad_mesh)
    grad_spec = to_columns(
        lax.all_to_all(grad_rows, "brick", split_axis=2, concat_axis=3, tiled=True)
    )
    state_rim = with_halo(state_bf, (("brick", 2),), 1)
    state_patch = patches(state_rim, 1, own_planes)
    conv_out = jnp.einsum(
        "tcyxz,tcd->dyxz", state_patch, conv_kernel, preferred_element_type=jnp.float32
    )
    mesh_mixed = state_bf.astype(jnp.float32) + conv_out
    mixed_rows = make_rows(mesh_mixed)
    state_spec = to_columns(
        lax.all_to_all(
            mixed_rows.astype(jnp.bfloat16), "brick", split_axis=2, concat_axis=3, tiled=True
        ).astype(mixed_rows.dtype)
    )
    products = jnp.sum(grad_spec[0] * state_spec[0] + grad_spec[1] * state_spec[1], axis=3)
    gain_part = jnp.transpose(products, (0, 2, 1)) / (NX * NY * math.sqrt(snap_count * NZ))
    gain_local = jnp.transpose(spectral_gain, (0, 2, 1))
    filtered = grad_spec * gain_local[None, :, :, :, None]
    before_cross = transform_columns(filtered, col_cosine, col_sine, -1.0)
    part_cols = lax.all_to_all(before_cross, "brick", split_axis=3, concat_axis=2, tiled=True)
    real_rows = jnp.einsum("ckxz,ky->cyxz", part_cols[0], row_cosine, precision=HIGHEST)
    imag_rows = jnp.einsum("ckxz,ky->cyxz", part_cols[1], row_sine, precision=HIGHEST)
    grad_mixed = (real_rows - imag_rows) / (NX * NY)
    grad_bf = grad_mixed.astype(jnp.bfloat16)
    flipped = conv_kernel[::-1]
    grad_padded = with_halo(grad_bf, (("brick", 2),), 1)
    grad_patch = patches(grad_padded, 1, own_planes)
    back_conv = jnp.einsum(
        "tdyxz,tcd->cyxz", grad_patch, flipped, preferred_element_type=jnp.float32
    )
    pulled = (grad_bf.astype(jnp.float32) + back_conv).astype(jnp.bfloat16)
    pulled_full = with_halo(pulled, (("brick", 2),), 1)
    kernel_part = jnp.einsum(
        "tcyxz,dyxz->tcd", state_patch, grad_bf, preferred_element_type=jnp.float32
    )
    kernel_part = kernel_part / math.sqrt(snap_count * NX * NY * NZ)
    pulled_tiles = pulled_full.reshape(channels, NY, tile_cells)
    atom_total = jnp.einsum(
        "ctj,tjs->cts", pulled_tiles, blocks, preferred_element_type=jnp.float32
    )
    atom_grad = atom_total.astype(jnp.bfloat16).reshape(1, channels, NY * slot_count)
    kernel_grad = lax.psum(kernel_part, ("snap", "brick"))
    gain_grad = lax.psum(gain_part, "snap")
    return (atom_grad, kernel_grad, gain_grad)


BF = jnp.bfloat16
F32 = jnp.float32
LANES = 128
ROWS = 8
PADX = 16
MESH = pl.DeviceIdType.MESH


def contract(left, right, dims, precision=None):
    return lax.dot_general(
        left, right, ((dims[:1], dims[1:]), ((), ())),
        precision=precision, preferred_element_type=F32,
    )


def vmem():
    return pl.BlockSpec(memory_space=pltpu.VMEM)


def shape_of(dims, kind):
    return jax.ShapeDtypeStruct(dims, kind)


def corner_block(index_ref, weight_ref, lanes, cell_of_row):
    block = jnp.zeros(cell_of_row.shape, F32)
    index = index_ref[:, lanes]
    weight = weight_ref[:, lanes]
    for corner in range(CORNERS):
        block = jnp.where(
            index[corner : corner + 1] == cell_of_row, weight[corner : corner + 1], block
        )
    return block.astype(BF)


def row_cells():
    row = lax.broadcasted_iota(jnp.int32, (NZ * PADX, LANES), 0)
    return (row % PADX) * NZ + row // PADX


def run_all(first, total, make):
    def go(step, carry):
        make(step).start()
        return carry

    lax.fori_loop(first, total, go, 0)


def wait_all(first, total, make):
    def finish(step, carry):
        make(step).wait()
        return carry

    lax.fori_loop(first, total, finish, 0)


def split(value):
    high = value.astype(BF)
    return high, (value - high.astype(F32)).astype(BF)


def three(left, right):
    left_high, left_low = left
    right_high, right_low = right
    return (
        contract(left_high, right_high, (1, 0))
        + contract(left_high, right_low, (1, 0))
        + contract(left_low, right_high, (1, 0))
    )


def widen(value):
    return jnp.concatenate(
        [jnp.roll(value, 1, axis=0), value, jnp.roll(value, -1, axis=0)], axis=1
    ).astype(BF)


def whole_body(
    bricks, snaps, chunks,
    feature_ref, cotangent_ref, index_ref, weight_ref, taps_ref, gain_ref,
    order_ref, rows_ref, cols_ref, inv_cols_ref, inv_rows_ref,
    atom_ref, kernel_ref, gain_out_ref,
    blocks, sums, edge, low, high, band, back_band, state, cat, grad_send, mixed_send,
    grad_slab, mixed_slab, gain_slab, field_f, back_f, spectra, ext, ret, back_cat, pulled,
    gain_send, gain_land, kernel_part, kernel_land, kernel_mine, kernel_all,
    edge_send, edge_recv, out_send, out_recv, ret_send, ret_recv,
    gain_ssem, gain_rsem, red_send, red_recv, own_sem,
):
    channels = feature_ref.shape[0]
    planes = NX // bricks
    per = channels // bricks
    total = bricks * snaps
    me = lax.axis_index("brick")
    side = lax.axis_index("snap")
    flat = side * bricks + me
    above = lax.rem(me + 1, bricks)
    below = lax.rem(me + bricks - 1, bricks)
    barrier = pltpu.get_barrier_semaphore()

    def device_of(step):
        other = lax.rem(flat + step, total)
        return other, {"snap": other // bricks, "brick": lax.rem(other, bricks)}

    def hello(step, carry):
        pl.semaphore_signal(barrier, inc=1, device_id=device_of(step)[1], device_id_type=MESH)
        return carry

    lax.fori_loop(1, total, hello, 0)

    def remote(src, dst, send_sem, recv_sem, device):
        return pltpu.make_async_remote_copy(
            src_ref=src, dst_ref=dst, send_sem=send_sem, recv_sem=recv_sem,
            device_id=device, device_id_type=MESH,
        )

    def local(src, dst):
        copy = pltpu.make_async_copy(src, dst, own_sem)
        copy.start()
        copy.wait()

    cells = row_cells()

    def spread_step(step, carry):
        parts = [[], []]
        for q in range(ROWS):
            y = step * ROWS + q
            lanes = pl.ds(pl.multiple_of(y * LANES, LANES), LANES)
            block = corner_block(index_ref, weight_ref, lanes, cells)
            blocks[y] = block
            stacked = jnp.concatenate([feature_ref[:, lanes], cotangent_ref[:, lanes]], axis=0)
            found = contract(block, stacked, (1, 1))
            for f in range(2):
                parts[f].append(
                    jnp.concatenate(
                        [
                            found[z * PADX : (z + 1) * PADX, f * channels : (f + 1) * channels]
                            for z in range(NZ)
                        ],
                        axis=1,
                    )
                )
        for f in range(2):
            turned = jnp.transpose(jnp.stack(parts[f]), (1, 0, 2))
            sums[f, :, pl.ds(pl.multiple_of(step * ROWS, ROWS), ROWS), :] = turned[: planes + 2]
        return carry

    def gain_copy(step):
        target = lax.rem(me + step, bricks)
        return remote(
            gain_ref.at[pl.ds(target * per, per)], gain_slab.at[:, me],
            out_send.at[2, step], out_recv.at[2, step], {"brick": target},
        )

    def edge_copy(chunk, way):
        rows = pl.ds(chunk * (NY // chunks), NY // chunks)
        land = low if way == 0 else high
        return remote(
            edge.at[pl.ds(3 * way, 3), rows], land.at[:, rows],
            edge_send.at[way, chunk], edge_recv.at[way, chunk],
            {"brick": above if way == 0 else below},
        )

    span = NY // chunks
    for chunk in range(chunks):
        lax.fori_loop(chunk * (span // ROWS), (chunk + 1) * (span // ROWS), spread_step, 0)
        rows = pl.ds(chunk * span, span)
        for slot, (f, plane) in enumerate(
            [(0, planes), (0, planes + 1), (1, planes + 1), (0, 0), (0, 1), (1, 0)]
        ):
            edge[slot, rows, :] = sums[f, plane, rows, :].astype(BF)
        if chunk == 0:
            pl.semaphore_wait(barrier, total - 1)
        for way in range(2):
            edge_copy(chunk, way).start()
    run_all(1, bricks, gain_copy)
    local(gain_ref.at[pl.ds(me * per, per)], gain_slab.at[:, me])

    lane = lax.broadcasted_iota(jnp.int32, (channels, LANES), 1) // channels
    for dx in range(3):
        for dy in range(3):
            tiled = []
            for dz in range(3):
                tap = taps_ref[9 * dx + 3 * dy + dz].astype(F32)
                tiled.append(jnp.concatenate([tap] * NZ, axis=1))
            lines = []
            for z in range(NZ):
                line = jnp.zeros((channels, LANES), F32)
                for dz in range(3):
                    line = jnp.where(lane == z - (dz - 1), tiled[dz], line)
                lines.append(line)
            square = jnp.concatenate(lines, axis=0)
            band[dx, dy * LANES : (dy + 1) * LANES, :] = square.astype(BF)
            back_band[2 - dx, (2 - dy) * LANES : (3 - dy) * LANES, :] = jnp.transpose(
                square, (1, 0)
            ).astype(BF)

    order = order_ref[...]

    def place(field, out, plane):
        turned = contract(order, field.astype(BF), (1, 1))
        out[plane] = turned.reshape(out.shape[1:]).astype(BF)

    def field_copy(kind, send, slab):
        def make(step):
            target = lax.rem(me + step, bricks)
            return remote(
                send.at[:, target], slab.at[pl.ds(me * planes, planes)],
                out_send.at[kind, step], out_recv.at[kind, step], {"brick": target},
            )

        return make

    grad_copy = field_copy(0, grad_send, grad_slab)
    mixed_copy = field_copy(1, mixed_send, mixed_slab)

    for plane in range(1, planes - 1):
        place(sums[1, plane + 1], grad_send, plane)
    for chunk in range(chunks):
        for way in range(2):
            edge_copy(chunk, way).wait()
    place(sums[1, 1] + low[2].astype(F32), grad_send, 0)
    place(sums[1, planes] + high[2].astype(F32), grad_send, planes - 1)
    run_all(1, bricks, grad_copy)
    local(grad_send.at[:, me], grad_slab.at[pl.ds(me * planes, planes)])

    for plane in range(planes + 2):
        value = sums[0, plane]
        if plane < 2:
            value = value + low[plane].astype(F32)
        if plane >= planes:
            value = value + high[plane - planes].astype(F32)
        rounded = value.astype(BF)
        state[plane] = rounded
        cat[plane] = widen(rounded.astype(F32))
    for plane in range(planes):
        value = state[plane + 1].astype(F32)
        for dx in range(3):
            value = value + contract(cat[plane + dx], band[dx], (1, 0))
        place(value, mixed_send, plane)
    run_all(1, bricks, mixed_copy)
    local(mixed_send.at[:, me], mixed_slab.at[pl.ds(me * planes, planes)])

    rows = rows_ref[...]
    cols = (cols_ref[0], cols_ref[1])
    inv_cols = (inv_cols_ref[0], inv_cols_ref[1])
    inv_rows = (inv_rows_ref[0], inv_rows_ref[1])

    def transform(channel):
        tall = jnp.concatenate([field_f[:, z * per + channel, :] for z in range(NZ)], axis=0)
        tall = tall.astype(BF)
        first = contract(jnp.concatenate([tall, tall], axis=1), rows, (1, 0))
        halves = []
        for half in range(2):
            halves.append(
                jnp.concatenate(
                    [
                        first[z * NX : (z + 1) * NX, half * NY : (half + 1) * NY]
                        for z in range(NZ)
                    ],
                    axis=1,
                )
            )
        return three(cols, split(jnp.concatenate(halves, axis=0)))

    wait_all(1, bricks, grad_copy)
    wait_all(1, bricks, gain_copy)
    field_f[...] = grad_slab[...].astype(F32)
    for channel in range(per):
        spectra[channel] = transform(channel)
        gain = jnp.transpose(gain_slab[channel].reshape(NY, NX), (1, 0))
        gain = jnp.concatenate([gain] * NZ, axis=1)
        gain = jnp.concatenate([gain, gain], axis=0)
        back = three(inv_cols, split(spectra[channel] * gain))
        flats = []
        for z in range(NZ):
            piece = back[:, z * NY : (z + 1) * NY]
            flats.append(jnp.concatenate([piece[:NX], piece[NX:]], axis=1))
        out = three(split(jnp.concatenate(flats, axis=0)), inv_rows) * (1.0 / (NX * NY))
        for z in range(NZ):
            back_f[:, z * per + channel, :] = out[z * NX : (z + 1) * NX]
    ext[pl.ds(2, NX)] = back_f[...].astype(BF)
    ext[pl.ds(0, 2)] = back_f[pl.ds(NX - 2, 2)].astype(BF)
    ext[pl.ds(NX + 2, 2)] = back_f[pl.ds(0, 2)].astype(BF)

    def ret_copy(step):
        target = lax.rem(me + step, bricks)
        return remote(
            ext.at[pl.ds(target * planes, planes + 4)], ret.at[:, me],
            ret_send.at[step], ret_recv.at[step], {"brick": target},
        )

    run_all(1, bricks, ret_copy)
    local(ext.at[pl.ds(me * planes, planes + 4)], ret.at[:, me])

    wait_all(1, bricks, mixed_copy)
    field_f[...] = mixed_slab[...].astype(F32)
    scale = 1.0 / (NX * NY * math.sqrt(snaps * NZ))
    for channel in range(per):
        product = spectra[channel] * transform(channel)
        product = product[:NX] + product[NX:]
        part = product[:, :NY]
        for z in range(1, NZ):
            part = part + product[:, z * NY : (z + 1) * NY]
        part = jnp.transpose(part * scale, (1, 0))
        gain_send[channel] = part.reshape(gain_send.shape[1:]).astype(gain_send.dtype)

    def part_copy(step):
        other, device = device_of(step)
        return remote(
            gain_send.at[:, lax.rem(other, bricks)], gain_land.at[side, pl.ds(me * per, per)],
            gain_ssem.at[step], gain_rsem.at[step], device,
        )

    wait_all(1, bricks, ret_copy)
    run_all(1, total, part_copy)
    local(gain_send.at[:, me], gain_land.at[side, pl.ds(me * per, per)])

    for plane in range(planes + 4):
        field = ret[plane].astype(F32).reshape(LANES, NY).astype(BF)
        back_cat[plane] = widen(contract(field, order, (0, 0)))
    own = back_cat[pl.ds(2, planes)].reshape(planes * NY, 3 * LANES)
    groups = [jnp.zeros((channels, LANES), F32) for _ in range(kernel_all.shape[0] * ROWS // channels)]
    tap_scale = 1.0 / math.sqrt(snaps * NX * NY * NZ)
    for dx in range(3):
        near = state[pl.ds(dx, planes)].reshape(planes * NY, LANES)
        gram = contract(near, own, (0, 0))
        for dy in range(3):
            square = gram[:, (2 - dy) * LANES : (3 - dy) * LANES]
            for dz in range(3):
                line = jnp.zeros((channels, LANES), F32)
                for z in range(NZ):
                    source = z + dz - 1
                    if 0 <= source < NZ:
                        line = jnp.where(
                            lane == z, square[source * channels : (source + 1) * channels], line
                        )
                line = line + pltpu.roll(line, LANES // 2, 1)
                line = line + pltpu.roll(line, LANES // 4, 1)
                tap = 9 * dx + 3 * dy + dz
                groups[tap // NZ] = jnp.where(
                    lane == tap % NZ, line * tap_scale, groups[tap // NZ]
                )
    tiles = channels // ROWS
    for position, value in enumerate(groups):
        kernel_part[position * tiles : (position + 1) * tiles] = value.reshape(tiles, ROWS, LANES)

    def scatter(step):
        other, device = device_of(step)
        return remote(
            kernel_part.at[other], kernel_land.at[flat],
            red_send.at[0, step], red_recv.at[0, step], device,
        )

    def share(step):
        _, device = device_of(step)
        return remote(
            kernel_mine, kernel_all.at[flat],
            red_send.at[1, step], red_recv.at[1, step], device,
        )

    run_all(1, total, scatter)
    local(kernel_part.at[flat], kernel_land.at[flat])

    for plane in range(planes + 2):
        value = back_cat[plane + 1, :, LANES : 2 * LANES].astype(F32)
        for dx in range(3):
            value = value + contract(back_cat[plane + dx], back_band[dx], (1, 0))
        pulled[plane] = value.astype(BF).astype(F32)
    for plane in range(planes + 2, PADX):
        pulled[plane] = jnp.zeros((NY, LANES), F32)

    wait_all(1, total, scatter)
    kernel_mine[...] = jnp.sum(kernel_land[...], axis=0)
    run_all(1, total, share)
    local(kernel_mine, kernel_all.at[flat])

    def gather_step(step, carry):
        here = pl.ds(pl.multiple_of(step * ROWS, ROWS), ROWS)
        turned = jnp.transpose(pulled[:, here, :], (1, 0, 2))
        for q in range(ROWS):
            y = step * ROWS + q
            lanes = pl.ds(pl.multiple_of(y * LANES, LANES), LANES)
            plane = turned[q]
            tall = jnp.concatenate(
                [plane[:, z * channels : (z + 1) * channels] for z in range(NZ)], axis=0
            )
            atom_ref[:, lanes] = contract(tall.astype(BF), blocks[y], (0, 0)).astype(BF)
        return carry

    lax.fori_loop(0, NY // ROWS, gather_step, 0)

    wait_all(1, total, part_copy)
    gain_sum = gain_land[0].astype(F32)
    for other in range(1, snaps):
        gain_sum = gain_sum + gain_land[other].astype(F32)
    gain_out_ref[...] = gain_sum
    wait_all(1, total, share)
    final = kernel_all[...].reshape(kernel_all.shape[0] * ROWS // channels, channels, LANES)
    for tap in range(kernel_ref.shape[0]):
        at = (tap % NZ) * channels
        kernel_ref[tap] = final[tap // NZ][:, at : at + channels]


def fast_shards(sizes, atom_features, cotangent, cell_index, assign_weight, conv_kernel, spectral_gain):
    snaps, bricks = sizes
    channels, atoms = atom_features.shape[1:]
    planes = NX // bricks
    per = channels // bricks
    group = NZ * per
    total = bricks * snaps
    chunks = 4
    order = np.zeros((LANES, LANES), np.float32)
    for brick in range(bricks):
        for z in range(NZ):
            for c in range(per):
                order[brick * group + z * per + c, z * channels + brick * per + c] = 1.0

    def angles(length):
        phase = np.outer(np.arange(length), np.arange(length)) % length
        turn = 2.0 * np.pi * phase / length
        return np.cos(turn), np.sin(turn)

    def halves(table):
        table = np.asarray(table, np.float32)
        high = table.astype(BF)
        low = (table - high.astype(np.float32)).astype(BF)
        return high, low

    col_cos, col_sin = angles(NX)
    row_cos, row_sin = angles(NY)
    rows = jnp.asarray(np.concatenate(halves(np.concatenate([row_cos, -row_sin], axis=1)), axis=0))
    cols = jnp.asarray(np.stack(halves(np.block([[col_cos, col_sin], [-col_sin, col_cos]]))))
    inv_cols = jnp.asarray(np.stack(halves(np.block([[col_cos, -col_sin], [col_sin, col_cos]]))))
    inv_rows = jnp.asarray(np.stack(halves(np.concatenate([row_cos, -row_sin], axis=0))))
    mesh_plane = (NY, LANES)
    send = (planes, bricks, group, NY)
    slab = (NX, group, NY)
    piece = (bricks, NY // bricks, NX)
    scratch = [
        ((NY, NZ * PADX, LANES), BF),
        ((2, planes + 2) + mesh_plane, F32),
        ((6,) + mesh_plane, BF),
        ((3,) + mesh_plane, BF),
        ((3,) + mesh_plane, BF),
        ((3, 3 * LANES, LANES), BF),
        ((3, 3 * LANES, LANES), BF),
        ((planes + 2,) + mesh_plane, BF),
        ((planes + 2, NY, 3 * LANES), BF),
        (send, BF),
        (send, BF),
        (slab, BF),
        (slab, BF),
        ((per,) + piece, F32),
        (slab, F32),
        (slab, F32),
        ((per, 2 * NX, NZ * NY), F32),
        ((NX + 4, group, NY), BF),
        ((planes + 4, bricks, group, NY), BF),
        ((planes + 4, NY, 3 * LANES), BF),
        ((PADX,) + mesh_plane, F32),
        ((per,) + piece, BF),
        ((snaps, channels) + piece[1:], BF),
        ((total, ROWS, LANES), F32),
        ((total, ROWS, LANES), F32),
        ((ROWS, LANES), F32),
        ((total, ROWS, LANES), F32),
    ]
    sems = [(2, chunks)] * 2 + [(3, bricks)] * 2 + [(bricks,)] * 2 + [(total,)] * 2 + [(2, total)] * 2
    atom_grad, kernel_grad, gain_grad = pl.pallas_call(
        lambda *refs: whole_body(bricks, snaps, chunks, *refs),
        out_shape=[
            shape_of((channels, atoms), BF),
            shape_of(conv_kernel.shape, F32),
            shape_of((channels,) + piece[1:], F32),
        ],
        in_specs=[vmem()] * 11,
        out_specs=[vmem()] * 3,
        scratch_shapes=[pltpu.VMEM(dims, kind) for dims, kind in scratch]
        + [pltpu.SemaphoreType.DMA(dims) for dims in sems]
        + [pltpu.SemaphoreType.DMA],
        compiler_params=pltpu.CompilerParams(
            collective_id=1, has_side_effects=True, vmem_limit_bytes=60 * 1024 * 1024
        ),
    )(
        atom_features[0], cotangent[0], cell_index[0], assign_weight[0], conv_kernel,
        jnp.transpose(spectral_gain, (0, 2, 1)), jnp.asarray(order, BF), rows, cols,
        inv_cols, inv_rows,
    )
    return (atom_grad[None], kernel_grad, jnp.transpose(gain_grad, (0, 2, 1)))


def fits(mesh, channels, atoms):
    bricks = mesh.shape["brick"]
    snaps = mesh.shape["snap"]
    return (
        channels * NZ == LANES
        and NX == LANES
        and NY == LANES
        and atoms // bricks == NY * LANES
        and channels % bricks == 0
        and NZ * channels // bricks == ROWS
        and NX // bricks == ROWS
        and 8 * channels == bricks * snaps * ROWS
    )


def solution(mesh):
    placed = (
        P("snap", None, "brick"),
        P("snap", None, "brick"),
        P("snap", None, "brick"),
        P("snap", None, "brick"),
        P(),
        P(None, None, "brick"),
    )
    sizes = (mesh.shape["snap"], mesh.shape["brick"])

    def pick(*arguments):
        if fits(mesh, arguments[0].shape[1], arguments[0].shape[2] * sizes[1]):
            return fast_shards(sizes, *arguments)
        return shards(*arguments)

    return jax.shard_map(
        pick,
        mesh=mesh,
        in_specs=placed,
        out_specs=(P("snap", None, "brick"), P(), P(None, None, "brick")),
        check_vma=False,
    )
```

profile of v0, /device:TPU:0, one launch (start us, length us, event | category | flops | bytes accessed | tf_op | source)
XLA Modules:
  0.0 62.6 jit_solution(2865453292015246145)
XLA Ops:
  0.6 58.0 %shard_map.130 = (bf16[32,16384]{1,0:T(8,128)(2,1)}, f32[27,32,32]{2,1,0:T(8,128)}, f32[32,8,128]{2,1,0:T(8,128)}) custom-call(bf16[32,16384]{1,0:T(8,128)(2,1)} %bitcast.8, bf16[32,16384]{1,0:T(8,128)(2,1)} %bitcast.9, s32[4,16384]{1,0:T(4,128)} %bitcast.10, f32[4,16384]{1,0:T(4,128)} %bitcast.11, bf16[27,32,32]{2,1,0:T(8,128)(2,1)} %refs_4_.1, ...), custom_call_target="tpu_custom_call" | custom-call | tf_op jit(solution)/shard_map/pallas_call | solution.py:638
  58.6 0.0 copy-start
  58.6 2.3 %copy.17 = bf16[1,32,16384]{2,1,0:T(8,128)(2,1)} copy(bf16[1,32,16384]{2,1,0:T(8,128)(2,1)} %bitcast.7) | data formatting | bytes 2097152
  60.9 0.0 copy-done
  61.0 0.0 copy-start.1
  61.0 0.8 %copy.18 = f32[27,32,32]{2,1,0:T(8,128)} copy(f32[27,32,32]{2,1,0:T(8,128)S(1)} %copy-done) | data formatting | bytes 221184
  61.7 0.3 copy-done.1
  62.0 0.7 %copy.19 = f32[32,128,8]{1,2,0:T(8,128)} copy(f32[32,128,8]{1,2,0:T(8,128)S(1)} %bitcast.12) | data formatting | bytes 262144
Async XLA Ops:
  58.6 2.3 %copy-start = (f32[27,32,32]{2,1,0:T(8,128)S(1)}, f32[27,32,32]{2,1,0:T(8,128)}, u32[]{:S(2)}) copy-start(f32[27,32,32]{2,1,0:T(8,128)} %get-tuple-element.13) | copy-start | bytes 331780
  61.0 1.0 %copy-start.1 = (f32[32,8,128]{2,1,0:T(8,128)S(1)}, f32[32,8,128]{2,1,0:T(8,128)}, u32[]{:S(2)}) copy-start(f32[32,8,128]{2,1,0:T(8,128)} %get-tuple-element.8) | copy-start | bytes 393220
where the time goes:
time: 62.8 us; the launch traced here: 62.6 us
  Pallas kernels  58 us (92%)
  local copies, waits for them, and re-layouts  4 us (6%)
  between operations  0.65 us (1%)
    pallas_call x1, Pallas kernels, fast_shards(): pl.pallas_call(lambda *refs: whole_body(bricks, snaps, chunks, *refs), ou...  58 us
    unnamed x7, local copies, waits for them, and re-layouts  4 us

commit v1 on v0

--- a/solution.py
+++ b/solution.py
@@ -246,14 +246,16 @@
 
 def whole_body(
     bricks, snaps, chunks,
+    feature_hbm, cotangent_hbm, index_hbm, weight_hbm, taps_hbm, gain_hbm,
+    order_hbm, rows_hbm, cols_hbm, inv_cols_hbm, inv_rows_hbm,
+    atom_ref, kernel_ref, gain_out_ref,
     feature_ref, cotangent_ref, index_ref, weight_ref, taps_ref, gain_ref,
     order_ref, rows_ref, cols_ref, inv_cols_ref, inv_rows_ref,
-    atom_ref, kernel_ref, gain_out_ref,
     blocks, sums, edge, low, high, band, back_band, state, cat, grad_send, mixed_send,
     grad_slab, mixed_slab, gain_slab, field_f, back_f, spectra, ext, ret, back_cat, pulled,
     gain_send, gain_land, kernel_part, kernel_land, kernel_mine, kernel_all,
     edge_send, edge_recv, out_send, out_recv, ret_send, ret_recv,
-    gain_ssem, gain_rsem, red_send, red_recv, own_sem,
+    gain_ssem, gain_rsem, red_send, red_recv, in_sem, table_sem,
 ):
     channels = feature_ref.shape[0]
     planes = NX // bricks
@@ -274,18 +276,52 @@
         pl.semaphore_signal(barrier, inc=1, device_id=device_of(step)[1], device_id_type=MESH)
         return carry
 
-    lax.fori_loop(1, total, hello, 0)
-
     def remote(src, dst, send_sem, recv_sem, device):
         return pltpu.make_async_remote_copy(
             src_ref=src, dst_ref=dst, send_sem=send_sem, recv_sem=recv_sem,
             device_id=device, device_id_type=MESH,
         )
 
-    def local(src, dst):
-        copy = pltpu.make_async_copy(src, dst, own_sem)
-        copy.start()
-        copy.wait()
+    half = bricks // 2
+
+    def partner(slot):
+        near = slot // half
+        offset = slot + near * (1 - half)
+        return lax.rem(me // half + 1 - near, 2) * half + lax.rem(me + offset, half)
+
+    span = NY // chunks
+    tables = [
+        pltpu.make_async_copy(src, dst, table_sem.at[number])
+        for number, (src, dst) in enumerate(
+            [
+                (gain_hbm, gain_ref), (order_hbm, order_ref), (taps_hbm, taps_ref),
+                (rows_hbm, rows_ref), (cols_hbm, cols_ref), (inv_cols_hbm, inv_cols_ref),
+                (inv_rows_hbm, inv_rows_ref),
+            ]
+        )
+    ]
+    loads = []
+    for chunk in range(chunks):
+        lanes = pl.ds(chunk * span * LANES, span * LANES)
+        loads.append(
+            [
+                pltpu.make_async_copy(src.at[:, lanes], dst.at[:, lanes], in_sem.at[number, chunk])
+                for number, (src, dst) in enumerate(
+                    [
+                        (index_hbm, index_ref), (weight_hbm, weight_ref),
+                        (feature_hbm, feature_ref), (cotangent_hbm, cotangent_ref),
+                    ]
+                )
+            ]
+        )
+    for load in loads[0]:
+        load.start()
+    lax.fori_loop(1, total, hello, 0)
+    for group in loads[1:]:
+        for load in group:
+            load.start()
+    for load in tables:
+        load.start()
 
     cells = row_cells()
 
@@ -313,37 +349,68 @@
             sums[f, :, pl.ds(pl.multiple_of(step * ROWS, ROWS), ROWS), :] = turned[: planes + 2]
         return carry
 
-    def gain_copy(step):
-        target = lax.rem(me + step, bricks)
+    def gain_copy(slot):
+        target = partner(slot)
         return remote(
             gain_ref.at[pl.ds(target * per, per)], gain_slab.at[:, me],
-            out_send.at[2, step], out_recv.at[2, step], {"brick": target},
-        )
-
-    def edge_copy(chunk, way):
-        rows = pl.ds(chunk * (NY // chunks), NY // chunks)
+            out_send.at[2, slot], out_recv.at[2, slot], {"brick": target},
+        )
+
+    def edge_copy(field, way):
+        first, count = (3 * way, 2) if field == 0 else (3 * way + 2, 1)
         land = low if way == 0 else high
         return remote(
-            edge.at[pl.ds(3 * way, 3), rows], land.at[:, rows],
-            edge_send.at[way, chunk], edge_recv.at[way, chunk],
+            edge.at[pl.ds(first, count)], land.at[pl.ds(first - 3 * way, count)],
+            edge_send.at[way, field], edge_recv.at[way, field],
             {"brick": above if way == 0 else below},
         )
 
-    span = NY // chunks
     for chunk in range(chunks):
+        for load in loads[chunk]:
+            load.wait()
+        if chunk == chunks - 1:
+            pl.semaphore_wait(barrier, total - 1)
+            tables[0].wait()
+            run_all(0, bricks - 1, gain_copy)
         lax.fori_loop(chunk * (span // ROWS), (chunk + 1) * (span // ROWS), spread_step, 0)
-        rows = pl.ds(chunk * span, span)
-        for slot, (f, plane) in enumerate(
-            [(0, planes), (0, planes + 1), (1, planes + 1), (0, 0), (0, 1), (1, 0)]
-        ):
-            edge[slot, rows, :] = sums[f, plane, rows, :].astype(BF)
-        if chunk == 0:
-            pl.semaphore_wait(barrier, total - 1)
+    for slot, (f, plane) in enumerate(
+        [(0, planes), (0, planes + 1), (1, planes + 1), (0, 0), (0, 1), (1, 0)]
+    ):
+        edge[slot] = sums[f, plane].astype(BF)
+    for field in (1, 0):
         for way in range(2):
-            edge_copy(chunk, way).start()
-    run_all(1, bricks, gain_copy)
-    local(gain_ref.at[pl.ds(me * per, per)], gain_slab.at[:, me])
-
+            edge_copy(field, way).start()
+
+    gain_slab[:, me] = gain_ref[pl.ds(me * per, per)]
+    tables[1].wait()
+    order = order_ref[...]
+    inner = planes - 2
+
+    def place(field, out, slot):
+        turned = contract(order, field.astype(BF), (1, 1))
+        out[slot] = turned.reshape(out.shape[1:]).astype(BF)
+
+    def field_copy(kind, send, slab, first, count):
+        def make(slot):
+            target = partner(slot)
+            return remote(
+                send.at[pl.ds(first, count), target],
+                slab.at[pl.ds(me * planes + first, count)],
+                out_send.at[kind, slot], out_recv.at[kind, slot], {"brick": target},
+            )
+
+        return make
+
+    grad_inner = field_copy(0, grad_send, grad_slab, 0, inner)
+    grad_outer = field_copy(3, grad_send, grad_slab, inner, 2)
+    mixed_copy = field_copy(1, mixed_send, mixed_slab, 0, planes)
+    slots = [inner] + list(range(inner)) + [inner + 1]
+
+    for plane in range(1, planes - 1):
+        place(sums[1, plane + 1], grad_send, slots[plane])
+    run_all(0, bricks - 1, grad_inner)
+
+    tables[2].wait()
     lane = lax.broadcasted_iota(jnp.int32, (channels, LANES), 1) // channels
     for dx in range(3):
         for dy in range(3):
@@ -363,35 +430,15 @@
                 square, (1, 0)
             ).astype(BF)
 
-    order = order_ref[...]
-
-    def place(field, out, plane):
-        turned = contract(order, field.astype(BF), (1, 1))
-        out[plane] = turned.reshape(out.shape[1:]).astype(BF)
-
-    def field_copy(kind, send, slab):
-        def make(step):
-            target = lax.rem(me + step, bricks)
-            return remote(
-                send.at[:, target], slab.at[pl.ds(me * planes, planes)],
-                out_send.at[kind, step], out_recv.at[kind, step], {"brick": target},
-            )
-
-        return make
-
-    grad_copy = field_copy(0, grad_send, grad_slab)
-    mixed_copy = field_copy(1, mixed_send, mixed_slab)
-
-    for plane in range(1, planes - 1):
-        place(sums[1, plane + 1], grad_send, plane)
-    for chunk in range(chunks):
-        for way in range(2):
-            edge_copy(chunk, way).wait()
-    place(sums[1, 1] + low[2].astype(F32), grad_send, 0)
-    place(sums[1, planes] + high[2].astype(F32), grad_send, planes - 1)
-    run_all(1, bricks, grad_copy)
-    local(grad_send.at[:, me], grad_slab.at[pl.ds(me * planes, planes)])
-
+    for way in range(2):
+        edge_copy(1, way).wait()
+    place(sums[1, 1] + low[2].astype(F32), grad_send, slots[0])
+    place(sums[1, planes] + high[2].astype(F32), grad_send, slots[planes - 1])
+    run_all(0, bricks - 1, grad_outer)
+    grad_slab[pl.ds(me * planes, planes)] = grad_send[:, me]
+
+    for way in range(2):
+        edge_copy(0, way).wait()
     for plane in range(planes + 2):
         value = sums[0, plane]
         if plane < 2:
@@ -405,9 +452,10 @@
         value = state[plane + 1].astype(F32)
         for dx in range(3):
             value = value + contract(cat[plane + dx], band[dx], (1, 0))
-        place(value, mixed_send, plane)
-    run_all(1, bricks, mixed_copy)
-    local(mixed_send.at[:, me], mixed_slab.at[pl.ds(me * planes, planes)])
+        place(value, mixed_send, slots[plane])
+    mixed_slab[pl.ds(me * planes, planes)] = mixed_send[:, me]
+    for load in tables[3:]:
+        load.wait()
 
     rows = rows_ref[...]
     cols = (cols_ref[0], cols_ref[1])
@@ -431,8 +479,9 @@
             )
         return three(cols, split(jnp.concatenate(halves, axis=0)))
 
-    wait_all(1, bricks, grad_copy)
-    wait_all(1, bricks, gain_copy)
+    wait_all(0, bricks - 1, gain_copy)
+    wait_all(0, bricks - 1, grad_inner)
+    wait_all(0, bricks - 1, grad_outer)
     field_f[...] = grad_slab[...].astype(F32)
     for channel in range(per):
         spectra[channel] = transform(channel)
@@ -451,38 +500,17 @@
     ext[pl.ds(0, 2)] = back_f[pl.ds(NX - 2, 2)].astype(BF)
     ext[pl.ds(NX + 2, 2)] = back_f[pl.ds(0, 2)].astype(BF)
 
-    def ret_copy(step):
-        target = lax.rem(me + step, bricks)
+    def ret_copy(slot):
+        target = partner(slot)
         return remote(
             ext.at[pl.ds(target * planes, planes + 4)], ret.at[:, me],
-            ret_send.at[step], ret_recv.at[step], {"brick": target},
-        )
-
-    run_all(1, bricks, ret_copy)
-    local(ext.at[pl.ds(me * planes, planes + 4)], ret.at[:, me])
-
-    wait_all(1, bricks, mixed_copy)
-    field_f[...] = mixed_slab[...].astype(F32)
-    scale = 1.0 / (NX * NY * math.sqrt(snaps * NZ))
-    for channel in range(per):
-        product = spectra[channel] * transform(channel)
-        product = product[:NX] + product[NX:]
-        part = product[:, :NY]
-        for z in range(1, NZ):
-            part = part + product[:, z * NY : (z + 1) * NY]
-        part = jnp.transpose(part * scale, (1, 0))
-        gain_send[channel] = part.reshape(gain_send.shape[1:]).astype(gain_send.dtype)
-
-    def part_copy(step):
-        other, device = device_of(step)
-        return remote(
-            gain_send.at[:, lax.rem(other, bricks)], gain_land.at[side, pl.ds(me * per, per)],
-            gain_ssem.at[step], gain_rsem.at[step], device,
-        )
-
-    wait_all(1, bricks, ret_copy)
-    run_all(1, total, part_copy)
-    local(gain_send.at[:, me], gain_land.at[side, pl.ds(me * per, per)])
+            ret_send.at[slot], ret_recv.at[slot], {"brick": target},
+        )
+
+    run_all(0, bricks - 1, ret_copy)
+    run_all(0, bricks - 1, mixed_copy)
+    ret[:, me] = ext[pl.ds(me * planes, planes + 4)]
+    wait_all(0, bricks - 1, ret_copy)
 
     for plane in range(planes + 4):
         field = ret[plane].astype(F32).reshape(LANES, NY).astype(BF)
@@ -528,7 +556,7 @@
         )
 
     run_all(1, total, scatter)
-    local(kernel_part.at[flat], kernel_land.at[flat])
+    kernel_land[flat] = kernel_part[flat]
 
     for plane in range(planes + 2):
         value = back_cat[plane + 1, :, LANES : 2 * LANES].astype(F32)
@@ -537,11 +565,6 @@
         pulled[plane] = value.astype(BF).astype(F32)
     for plane in range(planes + 2, PADX):
         pulled[plane] = jnp.zeros((NY, LANES), F32)
-
-    wait_all(1, total, scatter)
-    kernel_mine[...] = jnp.sum(kernel_land[...], axis=0)
-    run_all(1, total, share)
-    local(kernel_mine, kernel_all.at[flat])
 
     def gather_step(step, carry):
         here = pl.ds(pl.multiple_of(step * ROWS, ROWS), ROWS)
@@ -556,7 +579,37 @@
             atom_ref[:, lanes] = contract(tall.astype(BF), blocks[y], (0, 0)).astype(BF)
         return carry
 
-    lax.fori_loop(0, NY // ROWS, gather_step, 0)
+    steps = NY // ROWS
+    lax.fori_loop(0, steps // 2, gather_step, 0)
+
+    wait_all(0, bricks - 1, mixed_copy)
+    field_f[...] = mixed_slab[...].astype(F32)
+    scale = 1.0 / (NX * NY * math.sqrt(snaps * NZ))
+    for channel in range(per):
+        product = spectra[channel] * transform(channel)
+        product = product[:NX] + product[NX:]
+        part = product[:, :NY]
+        for z in range(1, NZ):
+            part = part + product[:, z * NY : (z + 1) * NY]
+        part = jnp.transpose(part * scale, (1, 0))
+        gain_send[channel] = part.reshape(gain_send.shape[1:]).astype(gain_send.dtype)
+
+    def part_copy(step):
+        other, device = device_of(step)
+        return remote(
+            gain_send.at[:, lax.rem(other, bricks)], gain_land.at[side, pl.ds(me * per, per)],
+            gain_ssem.at[step], gain_rsem.at[step], device,
+        )
+
+    run_all(1, total, part_copy)
+    gain_land[side, pl.ds(me * per, per)] = gain_send[:, me]
+
+    wait_all(1, total, scatter)
+    kernel_mine[...] = jnp.sum(kernel_land[...], axis=0)
+    run_all(1, total, share)
+    kernel_all[flat] = kernel_mine[...]
+
+    lax.fori_loop(steps // 2, steps, gather_step, 0)
 
     wait_all(1, total, part_copy)
     gain_sum = gain_land[0].astype(F32)
@@ -598,7 +651,10 @@
     col_cos, col_sin = angles(NX)
     row_cos, row_sin = angles(NY)
     rows = jnp.asarray(np.concatenate(halves(np.concatenate([row_cos, -row_sin], axis=1)), axis=0))
-    cols = jnp.asarray(np.stack(halves(np.block([[col_cos, col_sin], [-col_sin, col_cos]]))))
+    local = list(range(1, planes - 1)) + [0, planes - 1]
+    order_x = [brick * planes + plane for brick in range(bricks) for plane in local]
+    col_cos_x, col_sin_x = col_cos[:, order_x], col_sin[:, order_x]
+    cols = jnp.asarray(np.stack(halves(np.block([[col_cos_x, col_sin_x], [-col_sin_x, col_cos_x]]))))
     inv_cols = jnp.asarray(np.stack(halves(np.block([[col_cos, -col_sin], [col_sin, col_cos]]))))
     inv_rows = jnp.asarray(np.stack(halves(np.concatenate([row_cos, -row_sin], axis=0))))
     mesh_plane = (NY, LANES)
@@ -606,6 +662,17 @@
     slab = (NX, group, NY)
     piece = (bricks, NY // bricks, NX)
     scratch = [
+        ((channels, atoms), BF),
+        ((channels, atoms), BF),
+        ((CORNERS, atoms), jnp.int32),
+        ((CORNERS, atoms), F32),
+        (conv_kernel.shape, BF),
+        ((channels,) + piece[1:], F32),
+        (order.shape, BF),
+        (rows.shape, BF),
+        (cols.shape, BF),
+        (inv_cols.shape, BF),
+        (inv_rows.shape, BF),
         ((NY, NZ * PADX, LANES), BF),
         ((2, planes + 2) + mesh_plane, F32),
         ((6,) + mesh_plane, BF),
@@ -634,19 +701,19 @@
         ((ROWS, LANES), F32),
         ((total, ROWS, LANES), F32),
     ]
-    sems = [(2, chunks)] * 2 + [(3, bricks)] * 2 + [(bricks,)] * 2 + [(total,)] * 2 + [(2, total)] * 2
+    sems = [(2, 2)] * 2 + [(4, bricks)] * 2 + [(bricks,)] * 2 + [(total,)] * 2 + [(2, total)] * 2
+    sems = sems + [(4, chunks), (7,)]
     atom_grad, kernel_grad, gain_grad = pl.pallas_call(
         lambda *refs: whole_body(bricks, snaps, chunks, *refs),
         out_shape=[
-            shape_of((channels, atoms), BF),
-            shape_of(conv_kernel.shape, F32),
-            shape_of((channels,) + piece[1:], F32),
+            pltpu.VMEM((channels, atoms), BF),
+            pltpu.VMEM(conv_kernel.shape, F32),
+            pltpu.VMEM((channels,) + piece[1:], F32),
         ],
-        in_specs=[vmem()] * 11,
+        in_specs=[pl.BlockSpec(memory_space=pl.ANY)] * 11,
         out_specs=[vmem()] * 3,
         scratch_shapes=[pltpu.VMEM(dims, kind) for dims, kind in scratch]
-        + [pltpu.SemaphoreType.DMA(dims) for dims in sems]
-        + [pltpu.SemaphoreType.DMA],
+        + [pltpu.SemaphoreType.DMA(dims) for dims in sems],
         compiler_params=pltpu.CompilerParams(
             collective_id=1, has_side_effects=True, vmem_limit_bytes=60 * 1024 * 1024
         ),
@@ -667,6 +734,7 @@
         and NY == LANES
         and atoms // bricks == NY * LANES
         and channels % bricks == 0
+        and bricks % 2 == 0
         and NZ * channels // bricks == ROWS
         and NX // bricks == ROWS
         and 8 * channels == bricks * snaps * ROWS

time: 62.8 us -> 58.4 us (0.930)
  Pallas kernels: 58 us -> 55.2 us
  local copies, waits for them, and re-layouts: 4 us -> 2.39 us
    pallas_call x1, Pallas kernels: 58 us -> 55.2 us  [fast_shards(): pl.pallas_call(lambda *refs: whole_body(bricks, snaps, chunks, *refs), ou...]
    unnamed x7 -> x3, local copies, waits for them, and re-layouts: 4 us -> 2.39 us
where the time goes in v1:
time: 58.4 us; the launch traced here: 58.2 us
  Pallas kernels  55.2 us (95%)
  local copies, waits for them, and re-layouts  2.39 us (4%)
  between operations  0.64 us (1%)
    pallas_call x1, Pallas kernels, fast_shards(): pl.pallas_call(lambda *refs: whole_body(bricks, snaps, chunks, *refs), ou...  55.2 us
    unnamed x3, local copies, waits for them, and re-layouts  2.39 us

profile of v1, /device:TPU:0, one launch (start us, length us, event | category | flops | bytes accessed | tf_op | source)
XLA Modules:
  0.0 58.2 jit_solution(11753547221967922502)
XLA Ops:
  0.6 55.2 %shard_map.130 = (bf16[32,16384]{1,0:T(8,128)(2,1)S(1)}, f32[27,32,32]{2,1,0:T(8,128)S(1)}, f32[32,8,128]{2,1,0:T(8,128)S(1)}) custom-call(bf16[32,16384]{1,0:T(8,128)(2,1)} %bitcast.9, bf16[32,16384]{1,0:T(8,128)(2,1)} %bitcast.10, s32[4,16384]{1,0:T(4,128)} %bitcast.11, f32[4,16384]{1,0:T(4,128)} %bitcast.12, bf16[27,32,32]{2,1,0:T(8,128)(2,1)} %refs_4_.1, ...), custom_call_target="tpu_custom_call" | custom-call | tf_op jit(solution)/shard_map/pallas_call | solution.py:706
  55.9 1.0 %copy.17 = bf16[1,32,16384]{2,1,0:T(8,128)(2,1)} copy(bf16[1,32,16384]{2,1,0:T(8,128)(2,1)S(1)} %bitcast.7) | data formatting | bytes 2097152
  56.8 0.7 %copy.19 = f32[32,128,8]{1,2,0:T(8,128)} copy(f32[32,128,8]{1,2,0:T(8,128)S(1)} %bitcast.8) | data formatting | bytes 262144
  57.5 0.8 %copy.18 = f32[27,32,32]{2,1,0:T(8,128)} copy(f32[27,32,32]{2,1,0:T(8,128)S(1)} %get-tuple-element.10) | data formatting | bytes 221184

commit v2 on v1

--- a/solution.py
+++ b/solution.py
@@ -253,9 +253,10 @@
     order_ref, rows_ref, cols_ref, inv_cols_ref, inv_rows_ref,
     blocks, sums, edge, low, high, band, back_band, state, cat, grad_send, mixed_send,
     grad_slab, mixed_slab, gain_slab, field_f, back_f, spectra, ext, ret, back_cat, pulled,
-    gain_send, gain_land, kernel_part, kernel_land, kernel_mine, kernel_all,
-    edge_send, edge_recv, out_send, out_recv, ret_send, ret_recv,
-    gain_ssem, gain_rsem, red_send, red_recv, in_sem, table_sem,
+    gain_out, gain_send, gain_pair, gain_both, gain_land,
+    kernel_part, kernel_pair, kernel_both, kernel_land, kernel_mine, kernel_all,
+    edge_sems, grad_sems, mixed_sems, gain_sems, ret_sems, part_sems, pair_sems, red_sems,
+    in_sem, table_sem,
 ):
     channels = feature_ref.shape[0]
     planes = NX // bricks
@@ -282,13 +283,13 @@
             device_id=device, device_id_type=MESH,
         )
 
-    half = bricks // 2
-
     def partner(slot):
-        near = slot // half
-        offset = slot + near * (1 - half)
-        return lax.rem(me // half + 1 - near, 2) * half + lax.rem(me + offset, half)
-
+        return lax.rem(me + 1 + slot, bricks)
+
+    def wait_for(src, dst, sems):
+        remote(src, dst, sems[0], sems[1], {"brick": above}).wait()
+
+    others = pl.ds(0, bricks - 1)
     span = NY // chunks
     tables = [
         pltpu.make_async_copy(src, dst, table_sem.at[number])
@@ -317,10 +318,7 @@
     for load in loads[0]:
         load.start()
     lax.fori_loop(1, total, hello, 0)
-    for group in loads[1:]:
-        for load in group:
-            load.start()
-    for load in tables:
+    for load in loads[1]:
         load.start()
 
     cells = row_cells()
@@ -352,63 +350,61 @@
     def gain_copy(slot):
         target = partner(slot)
         return remote(
-            gain_ref.at[pl.ds(target * per, per)], gain_slab.at[:, me],
-            out_send.at[2, slot], out_recv.at[2, slot], {"brick": target},
-        )
-
-    def edge_copy(field, way):
-        first, count = (3 * way, 2) if field == 0 else (3 * way + 2, 1)
-        land = low if way == 0 else high
+            gain_out.at[pl.ds(target * per, per)], gain_slab.at[:, me],
+            gain_sems.at[0], gain_sems.at[1], {"brick": target},
+        )
+
+    def edge_copy(way):
         return remote(
-            edge.at[pl.ds(first, count)], land.at[pl.ds(first - 3 * way, count)],
-            edge_send.at[way, field], edge_recv.at[way, field],
-            {"brick": above if way == 0 else below},
+            edge.at[pl.ds(2 * way, 2)], low if way == 0 else high,
+            edge_sems.at[way, 0], edge_sems.at[way, 1], {"brick": above if way == 0 else below},
         )
 
     for chunk in range(chunks):
         for load in loads[chunk]:
             load.wait()
+        if chunk + 2 < chunks:
+            for load in loads[chunk + 2]:
+                load.start()
+        if chunk + 2 == chunks:
+            for load in tables:
+                load.start()
         if chunk == chunks - 1:
+            tables[0].wait()
+            gain_out[...] = gain_ref[...].astype(BF)
+            gain_slab[:, me] = gain_out[pl.ds(me * per, per)]
             pl.semaphore_wait(barrier, total - 1)
-            tables[0].wait()
             run_all(0, bricks - 1, gain_copy)
         lax.fori_loop(chunk * (span // ROWS), (chunk + 1) * (span // ROWS), spread_step, 0)
-    for slot, (f, plane) in enumerate(
-        [(0, planes), (0, planes + 1), (1, planes + 1), (0, 0), (0, 1), (1, 0)]
-    ):
-        edge[slot] = sums[f, plane].astype(BF)
-    for field in (1, 0):
-        for way in range(2):
-            edge_copy(field, way).start()
-
-    gain_slab[:, me] = gain_ref[pl.ds(me * per, per)]
+    for slot, plane in enumerate([planes, planes + 1, 0, 1]):
+        edge[slot] = sums[0, plane].astype(BF)
+
+    for way in range(2):
+        edge_copy(way).start()
     tables[1].wait()
     order = order_ref[...]
-    inner = planes - 2
-
-    def place(field, out, slot):
+
+    def place(field, out, plane):
         turned = contract(order, field.astype(BF), (1, 1))
-        out[slot] = turned.reshape(out.shape[1:]).astype(BF)
-
-    def field_copy(kind, send, slab, first, count):
+        out[plane] = turned.reshape(out.shape[1:]).astype(BF)
+
+    def field_copy(sems, send, slab):
         def make(slot):
             target = partner(slot)
             return remote(
-                send.at[pl.ds(first, count), target],
-                slab.at[pl.ds(me * planes + first, count)],
-                out_send.at[kind, slot], out_recv.at[kind, slot], {"brick": target},
+                send.at[:, target], slab.at[me],
+                sems.at[0], sems.at[1], {"brick": target},
             )
 
         return make
 
-    grad_inner = field_copy(0, grad_send, grad_slab, 0, inner)
-    grad_outer = field_copy(3, grad_send, grad_slab, inner, 2)
-    mixed_copy = field_copy(1, mixed_send, mixed_slab, 0, planes)
-    slots = [inner] + list(range(inner)) + [inner + 1]
-
-    for plane in range(1, planes - 1):
-        place(sums[1, plane + 1], grad_send, slots[plane])
-    run_all(0, bricks - 1, grad_inner)
+    grad_copy = field_copy(grad_sems, grad_send, grad_slab)
+    mixed_copy = field_copy(mixed_sems, mixed_send, mixed_slab)
+
+    for plane in range(planes + 2):
+        place(sums[1, plane], grad_send, plane)
+    run_all(0, bricks - 1, grad_copy)
+    grad_slab[me] = grad_send[:, me]
 
     tables[2].wait()
     lane = lax.broadcasted_iota(jnp.int32, (channels, LANES), 1) // channels
@@ -431,14 +427,7 @@
             ).astype(BF)
 
     for way in range(2):
-        edge_copy(1, way).wait()
-    place(sums[1, 1] + low[2].astype(F32), grad_send, slots[0])
-    place(sums[1, planes] + high[2].astype(F32), grad_send, slots[planes - 1])
-    run_all(0, bricks - 1, grad_outer)
-    grad_slab[pl.ds(me * planes, planes)] = grad_send[:, me]
-
-    for way in range(2):
-        edge_copy(0, way).wait()
+        edge_copy(way).wait()
     for plane in range(planes + 2):
         value = sums[0, plane]
         if plane < 2:
@@ -452,11 +441,13 @@
         value = state[plane + 1].astype(F32)
         for dx in range(3):
             value = value + contract(cat[plane + dx], band[dx], (1, 0))
-        place(value, mixed_send, slots[plane])
-    mixed_slab[pl.ds(me * planes, planes)] = mixed_send[:, me]
+        place(value, mixed_send, plane)
+
+    run_all(0, bricks - 1, mixed_copy)
+    mixed_slab[me] = mixed_send[:, me]
+
     for load in tables[3:]:
         load.wait()
-
     rows = rows_ref[...]
     cols = (cols_ref[0], cols_ref[1])
     inv_cols = (inv_cols_ref[0], inv_cols_ref[1])
@@ -479,13 +470,18 @@
             )
         return three(cols, split(jnp.concatenate(halves, axis=0)))
 
-    wait_all(0, bricks - 1, gain_copy)
-    wait_all(0, bricks - 1, grad_inner)
-    wait_all(0, bricks - 1, grad_outer)
-    field_f[...] = grad_slab[...].astype(F32)
+    wait_for(grad_send.at[:, others], grad_slab.at[others], (grad_sems.at[0], grad_sems.at[1]))
+    for brick in range(bricks):
+        field = grad_slab[brick].astype(F32)
+        before = grad_slab[(brick + bricks - 1) % bricks, planes + 1].astype(F32)
+        after = grad_slab[(brick + 1) % bricks, 0].astype(F32)
+        field_f[pl.ds(brick * planes, planes)] = field[1 : planes + 1]
+        field_f[brick * planes] = field[1] + before
+        field_f[(brick + 1) * planes - 1] = field[planes] + after
+    wait_for(gain_slab.at[:, others], gain_slab.at[:, others], (gain_sems.at[0], gain_sems.at[1]))
     for channel in range(per):
         spectra[channel] = transform(channel)
-        gain = jnp.transpose(gain_slab[channel].reshape(NY, NX), (1, 0))
+        gain = jnp.transpose(gain_slab[channel].astype(F32).reshape(NY, NX), (1, 0))
         gain = jnp.concatenate([gain] * NZ, axis=1)
         gain = jnp.concatenate([gain, gain], axis=0)
         back = three(inv_cols, split(spectra[channel] * gain))
@@ -504,14 +500,43 @@
         target = partner(slot)
         return remote(
             ext.at[pl.ds(target * planes, planes + 4)], ret.at[:, me],
-            ret_send.at[slot], ret_recv.at[slot], {"brick": target},
+            ret_sems.at[0], ret_sems.at[1], {"brick": target},
         )
 
     run_all(0, bricks - 1, ret_copy)
-    run_all(0, bricks - 1, mixed_copy)
     ret[:, me] = ext[pl.ds(me * planes, planes + 4)]
-    wait_all(0, bricks - 1, ret_copy)
-
+
+    wait_for(mixed_send.at[:, others], mixed_slab.at[others], (mixed_sems.at[0], mixed_sems.at[1]))
+    field_f[...] = mixed_slab[...].reshape(field_f.shape).astype(F32)
+    scale = 1.0 / (NX * NY * math.sqrt(snaps * NZ))
+    for channel in range(per):
+        product = spectra[channel] * transform(channel)
+        product = product[:NX] + product[NX:]
+        part = product[:, :NY]
+        for z in range(1, NZ):
+            part = part + product[:, z * NY : (z + 1) * NY]
+        part = jnp.transpose(part * scale, (1, 0))
+        gain_send[channel] = part.reshape(gain_send.shape[1:]).astype(gain_send.dtype)
+
+    def sibling(src, dst, sems):
+        return remote(src, dst, sems.at[0], sems.at[1], {"snap": snaps - 1 - side})
+
+    gain_swap = sibling(gain_send.at[1 - side], gain_pair, pair_sems.at[0])
+    gain_swap.start()
+    gain_swap.wait()
+    gain_both[...] = (gain_send[side] + gain_pair[...]).astype(BF)
+
+    def part_copy(step):
+        other, device = device_of(step)
+        return remote(
+            gain_both.at[lax.rem(other, bricks)], gain_land.at[me * per + side],
+            part_sems.at[0], part_sems.at[1], device,
+        )
+
+    run_all(1, total, part_copy)
+    gain_land[me * per + side] = gain_both[me]
+
+    wait_for(ret.at[:, others], ret.at[:, others], (ret_sems.at[0], ret_sems.at[1]))
     for plane in range(planes + 4):
         field = ret[plane].astype(F32).reshape(LANES, NY).astype(BF)
         back_cat[plane] = widen(contract(field, order, (0, 0)))
@@ -541,22 +566,23 @@
     for position, value in enumerate(groups):
         kernel_part[position * tiles : (position + 1) * tiles] = value.reshape(tiles, ROWS, LANES)
 
-    def scatter(step):
-        other, device = device_of(step)
+    tap_swap = sibling(
+        kernel_part.at[pl.ds((1 - side) * bricks, bricks)], kernel_pair, pair_sems.at[1]
+    )
+    tap_swap.start()
+
+    def scatter(slot):
+        target = partner(slot)
         return remote(
-            kernel_part.at[other], kernel_land.at[flat],
-            red_send.at[0, step], red_recv.at[0, step], device,
+            kernel_both.at[target], kernel_land.at[me],
+            red_sems.at[0, 0], red_sems.at[0, 1], {"brick": target},
         )
 
     def share(step):
         _, device = device_of(step)
         return remote(
-            kernel_mine, kernel_all.at[flat],
-            red_send.at[1, step], red_recv.at[1, step], device,
-        )
-
-    run_all(1, total, scatter)
-    kernel_land[flat] = kernel_part[flat]
+            kernel_mine, kernel_all.at[flat], red_sems.at[1, 0], red_sems.at[1, 1], device,
+        )
 
     for plane in range(planes + 2):
         value = back_cat[plane + 1, :, LANES : 2 * LANES].astype(F32)
@@ -565,6 +591,11 @@
         pulled[plane] = value.astype(BF).astype(F32)
     for plane in range(planes + 2, PADX):
         pulled[plane] = jnp.zeros((NY, LANES), F32)
+
+    tap_swap.wait()
+    kernel_both[...] = kernel_part[pl.ds(side * bricks, bricks)] + kernel_pair[...]
+    run_all(0, bricks - 1, scatter)
+    kernel_land[me] = kernel_both[me]
 
     def gather_step(step, carry):
         here = pl.ds(pl.multiple_of(step * ROWS, ROWS), ROWS)
@@ -582,42 +613,18 @@
     steps = NY // ROWS
     lax.fori_loop(0, steps // 2, gather_step, 0)
 
-    wait_all(0, bricks - 1, mixed_copy)
-    field_f[...] = mixed_slab[...].astype(F32)
-    scale = 1.0 / (NX * NY * math.sqrt(snaps * NZ))
-    for channel in range(per):
-        product = spectra[channel] * transform(channel)
-        product = product[:NX] + product[NX:]
-        part = product[:, :NY]
-        for z in range(1, NZ):
-            part = part + product[:, z * NY : (z + 1) * NY]
-        part = jnp.transpose(part * scale, (1, 0))
-        gain_send[channel] = part.reshape(gain_send.shape[1:]).astype(gain_send.dtype)
-
-    def part_copy(step):
-        other, device = device_of(step)
-        return remote(
-            gain_send.at[:, lax.rem(other, bricks)], gain_land.at[side, pl.ds(me * per, per)],
-            gain_ssem.at[step], gain_rsem.at[step], device,
-        )
-
-    run_all(1, total, part_copy)
-    gain_land[side, pl.ds(me * per, per)] = gain_send[:, me]
-
-    wait_all(1, total, scatter)
-    kernel_mine[...] = jnp.sum(kernel_land[...], axis=0)
+    wait_for(kernel_land.at[others], kernel_land.at[others], (red_sems.at[0, 0], red_sems.at[0, 1]))
+    kernel_mine[...] = jnp.sum(kernel_land[...], axis=0).astype(BF)
     run_all(1, total, share)
     kernel_all[flat] = kernel_mine[...]
 
     lax.fori_loop(steps // 2, steps, gather_step, 0)
 
-    wait_all(1, total, part_copy)
-    gain_sum = gain_land[0].astype(F32)
-    for other in range(1, snaps):
-        gain_sum = gain_sum + gain_land[other].astype(F32)
-    gain_out_ref[...] = gain_sum
-    wait_all(1, total, share)
-    final = kernel_all[...].reshape(kernel_all.shape[0] * ROWS // channels, channels, LANES)
+    rest = pl.ds(0, total - 1)
+    wait_for(gain_land.at[rest], gain_land.at[rest], (part_sems.at[0], part_sems.at[1]))
+    gain_out_ref[...] = gain_land[...].astype(F32)
+    wait_for(kernel_all.at[rest], kernel_all.at[rest], (red_sems.at[1, 0], red_sems.at[1, 1]))
+    final = kernel_all[...].astype(F32).reshape(kernel_all.shape[0] * ROWS // channels, channels, LANES)
     for tap in range(kernel_ref.shape[0]):
         at = (tap % NZ) * channels
         kernel_ref[tap] = final[tap // NZ][:, at : at + channels]
@@ -651,10 +658,7 @@
     col_cos, col_sin = angles(NX)
     row_cos, row_sin = angles(NY)
     rows = jnp.asarray(np.concatenate(halves(np.concatenate([row_cos, -row_sin], axis=1)), axis=0))
-    local = list(range(1, planes - 1)) + [0, planes - 1]
-    order_x = [brick * planes + plane for brick in range(bricks) for plane in local]
-    col_cos_x, col_sin_x = col_cos[:, order_x], col_sin[:, order_x]
-    cols = jnp.asarray(np.stack(halves(np.block([[col_cos_x, col_sin_x], [-col_sin_x, col_cos_x]]))))
+    cols = jnp.asarray(np.stack(halves(np.block([[col_cos, col_sin], [-col_sin, col_cos]]))))
     inv_cols = jnp.asarray(np.stack(halves(np.block([[col_cos, -col_sin], [col_sin, col_cos]]))))
     inv_rows = jnp.asarray(np.stack(halves(np.concatenate([row_cos, -row_sin], axis=0))))
     mesh_plane = (NY, LANES)
@@ -675,18 +679,18 @@
         (inv_rows.shape, BF),
         ((NY, NZ * PADX, LANES), BF),
         ((2, planes + 2) + mesh_plane, F32),
-        ((6,) + mesh_plane, BF),
-        ((3,) + mesh_plane, BF),
-        ((3,) + mesh_plane, BF),
+        ((4,) + mesh_plane, BF),
+        ((2,) + mesh_plane, BF),
+        ((2,) + mesh_plane, BF),
         ((3, 3 * LANES, LANES), BF),
         ((3, 3 * LANES, LANES), BF),
         ((planes + 2,) + mesh_plane, BF),
         ((planes + 2, NY, 3 * LANES), BF),
+        ((planes + 2,) + send[1:], BF),
         (send, BF),
-        (send, BF),
-        (slab, BF),
-        (slab, BF),
-        ((per,) + piece, F32),
+        ((bricks, planes + 2) + slab[1:], BF),
+        ((bricks, planes) + slab[1:], BF),
+        ((per,) + piece, BF),
         (slab, F32),
         (slab, F32),
         ((per, 2 * NX, NZ * NY), F32),
@@ -694,15 +698,19 @@
         ((planes + 4, bricks, group, NY), BF),
         ((planes + 4, NY, 3 * LANES), BF),
         ((PADX,) + mesh_plane, F32),
-        ((per,) + piece, BF),
-        ((snaps, channels) + piece[1:], BF),
+        ((channels,) + piece[1:], BF),
+        ((per,) + piece, F32),
+        (piece, F32),
+        (piece, BF),
+        ((channels,) + piece[1:], BF),
         ((total, ROWS, LANES), F32),
-        ((total, ROWS, LANES), F32),
-        ((ROWS, LANES), F32),
-        ((total, ROWS, LANES), F32),
+        ((bricks, ROWS, LANES), F32),
+        ((bricks, ROWS, LANES), F32),
+        ((bricks, ROWS, LANES), F32),
+        ((ROWS, LANES), BF),
+        ((total, ROWS, LANES), BF),
     ]
-    sems = [(2, 2)] * 2 + [(4, bricks)] * 2 + [(bricks,)] * 2 + [(total,)] * 2 + [(2, total)] * 2
-    sems = sems + [(4, chunks), (7,)]
+    sems = [(2, 2)] + [(2,)] * 5 + [(2, 2)] * 2 + [(4, chunks), (7,)]
     atom_grad, kernel_grad, gain_grad = pl.pallas_call(
         lambda *refs: whole_body(bricks, snaps, chunks, *refs),
         out_shape=[
@@ -734,7 +742,7 @@
         and NY == LANES
         and atoms // bricks == NY * LANES
         and channels % bricks == 0
-        and bricks % 2 == 0
+        and snaps == 2
         and NZ * channels // bricks == ROWS
         and NX // bricks == ROWS
         and 8 * channels == bricks * snaps * ROWS

time: 58.4 us -> 50.2 us (0.86)
  Pallas kernels: 55.2 us -> 47 us
    pallas_call x1, Pallas kernels: 55.2 us -> 47 us  [fast_shards(): pl.pallas_call(lambda *refs: whole_body(bricks, snaps, chunks, *refs), ou...]
where the time goes in v2:
time: 50.2 us; the launch traced here: 50.1 us
  Pallas kernels  47 us (94%)
  local copies, waits for them, and re-layouts  2.39 us (5%)
  between operations  0.64 us (1%)
    pallas_call x1, Pallas kernels, fast_shards(): pl.pallas_call(lambda *refs: whole_body(bricks, snaps, chunks, *refs), ou...  47 us
    unnamed x3, local copies, waits for them, and re-layouts  2.39 us

profile of v2, /device:TPU:0, one launch (start us, length us, event | category | flops | bytes accessed | tf_op | source)
XLA Modules:
  0.0 50.1 jit_solution(4292023625092982325)
XLA Ops:
  0.6 47.0 %shard_map.130 = (bf16[32,16384]{1,0:T(8,128)(2,1)S(1)}, f32[27,32,32]{2,1,0:T(8,128)S(1)}, f32[32,8,128]{2,1,0:T(8,128)S(1)}) custom-call(bf16[32,16384]{1,0:T(8,128)(2,1)} %bitcast.9, bf16[32,16384]{1,0:T(8,128)(2,1)} %bitcast.10, s32[4,16384]{1,0:T(4,128)} %bitcast.11, f32[4,16384]{1,0:T(4,128)} %bitcast.12, bf16[27,32,32]{2,1,0:T(8,128)(2,1)} %refs_4_.1, ...), custom_call_target="tpu_custom_call" | custom-call | tf_op jit(solution)/shard_map/pallas_call | solution.py:714
  47.7 1.0 %copy.17 = bf16[1,32,16384]{2,1,0:T(8,128)(2,1)} copy(bf16[1,32,16384]{2,1,0:T(8,128)(2,1)S(1)} %bitcast.7) | data formatting | bytes 2097152
  48.7 0.7 %copy.19 = f32[32,128,8]{1,2,0:T(8,128)} copy(f32[32,128,8]{1,2,0:T(8,128)S(1)} %bitcast.8) | data formatting | bytes 262144
  49.3 0.8 %copy.18 = f32[27,32,32]{2,1,0:T(8,128)} copy(f32[27,32,32]{2,1,0:T(8,128)S(1)} %get-tuple-element.10) | data formatting | bytes 221184

commit v3 on v2

--- a/solution.py
+++ b/solution.py
@@ -253,8 +253,8 @@
     order_ref, rows_ref, cols_ref, inv_cols_ref, inv_rows_ref,
     blocks, sums, edge, low, high, band, back_band, state, cat, grad_send, mixed_send,
     grad_slab, mixed_slab, gain_slab, field_f, back_f, spectra, ext, ret, back_cat, pulled,
-    gain_out, gain_send, gain_pair, gain_both, gain_land,
-    kernel_part, kernel_pair, kernel_both, kernel_land, kernel_mine, kernel_all,
+    gain_out, gain_send, gain_pair, gain_both, part_all,
+    kernel_part, kernel_land, kernel_mine, kernel_all,
     edge_sems, grad_sems, mixed_sems, gain_sems, ret_sems, part_sems, pair_sems, red_sems,
     in_sem, table_sem,
 ):
@@ -399,7 +399,18 @@
         return make
 
     grad_copy = field_copy(grad_sems, grad_send, grad_slab)
-    mixed_copy = field_copy(mixed_sems, mixed_send, mixed_slab)
+    def mixed_copy(first, count):
+        some = pl.ds(first, count)
+
+        def make(slot):
+            target = partner(slot)
+            return remote(
+                mixed_send.at[some, target], mixed_slab.at[me, some],
+                mixed_sems.at[0], mixed_sems.at[1], {"brick": target},
+            )
+
+        return make
+
 
     for plane in range(planes + 2):
         place(sums[1, plane], grad_send, plane)
@@ -426,24 +437,31 @@
                 square, (1, 0)
             ).astype(BF)
 
-    for way in range(2):
-        edge_copy(way).wait()
-    for plane in range(planes + 2):
-        value = sums[0, plane]
-        if plane < 2:
-            value = value + low[plane].astype(F32)
-        if plane >= planes:
-            value = value + high[plane - planes].astype(F32)
+    def settle(plane, value):
         rounded = value.astype(BF)
         state[plane] = rounded
         cat[plane] = widen(rounded.astype(F32))
-    for plane in range(planes):
+
+    def convolve(plane):
         value = state[plane + 1].astype(F32)
         for dx in range(3):
             value = value + contract(cat[plane + dx], band[dx], (1, 0))
         place(value, mixed_send, plane)
 
-    run_all(0, bricks - 1, mixed_copy)
+    for plane in range(2, planes):
+        settle(plane, sums[0, plane])
+    for plane in range(2, planes - 2):
+        convolve(plane)
+    run_all(0, bricks - 1, mixed_copy(2, planes - 4))
+    for way in range(2):
+        edge_copy(way).wait()
+    for plane in range(2):
+        settle(plane, sums[0, plane] + low[plane].astype(F32))
+        settle(planes + plane, sums[0, planes + plane] + high[plane].astype(F32))
+    for plane in (0, 1, planes - 2, planes - 1):
+        convolve(plane)
+    run_all(0, bricks - 1, mixed_copy(0, 2))
+    run_all(0, bricks - 1, mixed_copy(planes - 2, 2))
     mixed_slab[me] = mixed_send[:, me]
 
     for load in tables[3:]:
@@ -518,23 +536,12 @@
         part = jnp.transpose(part * scale, (1, 0))
         gain_send[channel] = part.reshape(gain_send.shape[1:]).astype(gain_send.dtype)
 
-    def sibling(src, dst, sems):
-        return remote(src, dst, sems.at[0], sems.at[1], {"snap": snaps - 1 - side})
-
-    gain_swap = sibling(gain_send.at[1 - side], gain_pair, pair_sems.at[0])
-    gain_swap.start()
-    gain_swap.wait()
-    gain_both[...] = (gain_send[side] + gain_pair[...]).astype(BF)
-
     def part_copy(step):
         other, device = device_of(step)
         return remote(
-            gain_both.at[lax.rem(other, bricks)], gain_land.at[me * per + side],
+            gain_send.at[other // bricks, lax.rem(other, bricks)], part_all.at[flat],
             part_sems.at[0], part_sems.at[1], device,
         )
-
-    run_all(1, total, part_copy)
-    gain_land[me * per + side] = gain_both[me]
 
     wait_for(ret.at[:, others], ret.at[:, others], (ret_sems.at[0], ret_sems.at[1]))
     for plane in range(planes + 4):
@@ -564,18 +571,15 @@
                 )
     tiles = channels // ROWS
     for position, value in enumerate(groups):
-        kernel_part[position * tiles : (position + 1) * tiles] = value.reshape(tiles, ROWS, LANES)
-
-    tap_swap = sibling(
-        kernel_part.at[pl.ds((1 - side) * bricks, bricks)], kernel_pair, pair_sems.at[1]
-    )
-    tap_swap.start()
-
-    def scatter(slot):
-        target = partner(slot)
+        kernel_part[position * tiles : (position + 1) * tiles] = value.reshape(
+            tiles, ROWS, LANES
+        ).astype(BF)
+
+    def scatter(step):
+        other, device = device_of(step)
         return remote(
-            kernel_both.at[target], kernel_land.at[me],
-            red_sems.at[0, 0], red_sems.at[0, 1], {"brick": target},
+            kernel_part.at[other], kernel_land.at[flat],
+            red_sems.at[0, 0], red_sems.at[0, 1], device,
         )
 
     def share(step):
@@ -583,6 +587,12 @@
         return remote(
             kernel_mine, kernel_all.at[flat], red_sems.at[1, 0], red_sems.at[1, 1], device,
         )
+
+    run_all(1, total, scatter)
+    kernel_land[flat] = kernel_part[flat]
+    run_all(1, total, part_copy)
+    part_all[flat] = gain_send[side, me]
+    rest = pl.ds(0, total - 1)
 
     for plane in range(planes + 2):
         value = back_cat[plane + 1, :, LANES : 2 * LANES].astype(F32)
@@ -591,11 +601,6 @@
         pulled[plane] = value.astype(BF).astype(F32)
     for plane in range(planes + 2, PADX):
         pulled[plane] = jnp.zeros((NY, LANES), F32)
-
-    tap_swap.wait()
-    kernel_both[...] = kernel_part[pl.ds(side * bricks, bricks)] + kernel_pair[...]
-    run_all(0, bricks - 1, scatter)
-    kernel_land[me] = kernel_both[me]
 
     def gather_step(step, carry):
         here = pl.ds(pl.multiple_of(step * ROWS, ROWS), ROWS)
@@ -613,16 +618,24 @@
     steps = NY // ROWS
     lax.fori_loop(0, steps // 2, gather_step, 0)
 
-    wait_for(kernel_land.at[others], kernel_land.at[others], (red_sems.at[0, 0], red_sems.at[0, 1]))
-    kernel_mine[...] = jnp.sum(kernel_land[...], axis=0).astype(BF)
+    wait_for(kernel_land.at[rest], kernel_land.at[rest], (red_sems.at[0, 0], red_sems.at[0, 1]))
+    kernel_mine[...] = jnp.sum(kernel_land[...].astype(F32), axis=0).astype(BF)
     run_all(1, total, share)
     kernel_all[flat] = kernel_mine[...]
 
+    wait_for(part_all.at[rest], part_all.at[rest], (part_sems.at[0], part_sems.at[1]))
+    gain_both[...] = part_all[pl.ds(0, bricks)].astype(F32) + part_all[pl.ds(bricks, bricks)].astype(F32)
+    gain_swap = remote(
+        gain_both, gain_pair, pair_sems.at[0], pair_sems.at[1], {"snap": snaps - 1 - side}
+    )
+    gain_swap.start()
+
     lax.fori_loop(steps // 2, steps, gather_step, 0)
 
-    rest = pl.ds(0, total - 1)
-    wait_for(gain_land.at[rest], gain_land.at[rest], (part_sems.at[0], part_sems.at[1]))
-    gain_out_ref[...] = gain_land[...].astype(F32)
+    gain_swap.wait()
+    for brick in range(bricks):
+        gain_out_ref[brick * per + side] = gain_both[brick]
+        gain_out_ref[brick * per + 1 - side] = gain_pair[brick]
     wait_for(kernel_all.at[rest], kernel_all.at[rest], (red_sems.at[1, 0], red_sems.at[1, 1]))
     final = kernel_all[...].astype(F32).reshape(kernel_all.shape[0] * ROWS // channels, channels, LANES)
     for tap in range(kernel_ref.shape[0]):
@@ -699,18 +712,16 @@
         ((planes + 4, NY, 3 * LANES), BF),
         ((PADX,) + mesh_plane, F32),
         ((channels,) + piece[1:], BF),
-        ((per,) + piece, F32),
+        ((per,) + piece, BF),
         (piece, F32),
-        (piece, BF),
-        ((channels,) + piece[1:], BF),
-        ((total, ROWS, LANES), F32),
-        ((bricks, ROWS, LANES), F32),
-        ((bricks, ROWS, LANES), F32),
-        ((bricks, ROWS, LANES), F32),
+        (piece, F32),
+        ((total,) + piece[1:], BF),
+        ((total, ROWS, LANES), BF),
+        ((total, ROWS, LANES), BF),
         ((ROWS, LANES), BF),
         ((total, ROWS, LANES), BF),
     ]
-    sems = [(2, 2)] + [(2,)] * 5 + [(2, 2)] * 2 + [(4, chunks), (7,)]
+    sems = [(2, 2)] + [(2,)] * 6 + [(2, 2)] + [(4, chunks), (7,)]
     atom_grad, kernel_grad, gain_grad = pl.pallas_call(
         lambda *refs: whole_body(bricks, snaps, chunks, *refs),
         out_shape=[

time: 50.2 us -> 49.7 us (0.990)
    pallas_call x1, Pallas kernels: 47 us -> 46.5 us  [fast_shards(): pl.pallas_call(lambda *refs: whole_body(bricks, snaps, chunks, *refs), ou...]
where the time goes in v3:
time: 49.7 us; the launch traced here: 49.5 us
  Pallas kernels  46.5 us (94%)
  local copies, waits for them, and re-layouts  2.39 us (5%)
  between operations  0.64 us (1%)
    pallas_call x1, Pallas kernels, fast_shards(): pl.pallas_call(lambda *refs: whole_body(bricks, snaps, chunks, *refs), ou...  46.5 us
    unnamed x3, local copies, waits for them, and re-layouts  2.39 us

profile of v3, /device:TPU:0, one launch (start us, length us, event | category | flops | bytes accessed | tf_op | source)
XLA Modules:
  0.0 49.5 jit_solution(9705334978320262378)
XLA Ops:
  0.6 46.5 %shard_map.130 = (bf16[32,16384]{1,0:T(8,128)(2,1)S(1)}, f32[27,32,32]{2,1,0:T(8,128)S(1)}, f32[32,8,128]{2,1,0:T(8,128)S(1)}) custom-call(bf16[32,16384]{1,0:T(8,128)(2,1)} %bitcast.9, bf16[32,16384]{1,0:T(8,128)(2,1)} %bitcast.10, s32[4,16384]{1,0:T(4,128)} %bitcast.11, f32[4,16384]{1,0:T(4,128)} %bitcast.12, bf16[27,32,32]{2,1,0:T(8,128)(2,1)} %refs_4_.1, ...), custom_call_target="tpu_custom_call" | custom-call | tf_op jit(solution)/shard_map/pallas_call | solution.py:725
  47.2 1.0 %copy.17 = bf16[1,32,16384]{2,1,0:T(8,128)(2,1)} copy(bf16[1,32,16384]{2,1,0:T(8,128)(2,1)S(1)} %bitcast.7) | data formatting | bytes 2097152
  48.1 0.7 %copy.19 = f32[32,128,8]{1,2,0:T(8,128)} copy(f32[32,128,8]{1,2,0:T(8,128)S(1)} %bitcast.8) | data formatting | bytes 262144
  48.8 0.8 %copy.18 = f32[27,32,32]{2,1,0:T(8,128)} copy(f32[27,32,32]{2,1,0:T(8,128)S(1)} %get-tuple-element.10) | data formatting | bytes 221184

commit v4 on v3

--- a/solution.py
+++ b/solution.py
@@ -616,7 +616,7 @@
         return carry
 
     steps = NY // ROWS
-    lax.fori_loop(0, steps // 2, gather_step, 0)
+    lax.fori_loop(0, steps // 4, gather_step, 0)
 
     wait_for(kernel_land.at[rest], kernel_land.at[rest], (red_sems.at[0, 0], red_sems.at[0, 1]))
     kernel_mine[...] = jnp.sum(kernel_land[...].astype(F32), axis=0).astype(BF)
@@ -630,7 +630,7 @@
     )
     gain_swap.start()
 
-    lax.fori_loop(steps // 2, steps, gather_step, 0)
+    lax.fori_loop(steps // 4, steps, gather_step, 0)
 
     gain_swap.wait()
     for brick in range(bricks):

time: 49.7 us -> 49.3 us (level)
  no operation moved by 1% of the time
where the time goes in v4:
time: 49.3 us; the launch traced here: 49.2 us
  Pallas kernels  46.2 us (94%)
  local copies, waits for them, and re-layouts  2.39 us (5%)
  between operations  0.64 us (1%)
    pallas_call x1, Pallas kernels, fast_shards(): pl.pallas_call(lambda *refs: whole_body(bricks, snaps, chunks, *refs), ou...  46.2 us
    unnamed x3, local copies, waits for them, and re-layouts  2.39 us

profile of v4, /device:TPU:0, one launch (start us, length us, event | category | flops | bytes accessed | tf_op | source)
XLA Modules:
  0.0 49.2 jit_solution(10250497392518437024)
XLA Ops:
  0.6 46.2 %shard_map.130 = (bf16[32,16384]{1,0:T(8,128)(2,1)S(1)}, f32[27,32,32]{2,1,0:T(8,128)S(1)}, f32[32,8,128]{2,1,0:T(8,128)S(1)}) custom-call(bf16[32,16384]{1,0:T(8,128)(2,1)} %bitcast.9, bf16[32,16384]{1,0:T(8,128)(2,1)} %bitcast.10, s32[4,16384]{1,0:T(4,128)} %bitcast.11, f32[4,16384]{1,0:T(4,128)} %bitcast.12, bf16[27,32,32]{2,1,0:T(8,128)(2,1)} %refs_4_.1, ...), custom_call_target="tpu_custom_call" | custom-call | tf_op jit(solution)/shard_map/pallas_call | solution.py:725
  46.8 1.0 %copy.17 = bf16[1,32,16384]{2,1,0:T(8,128)(2,1)} copy(bf16[1,32,16384]{2,1,0:T(8,128)(2,1)S(1)} %bitcast.7) | data formatting | bytes 2097152
  47.8 0.7 %copy.19 = f32[32,128,8]{1,2,0:T(8,128)} copy(f32[32,128,8]{1,2,0:T(8,128)S(1)} %bitcast.8) | data formatting | bytes 262144
  48.4 0.8 %copy.18 = f32[27,32,32]{2,1,0:T(8,128)} copy(f32[27,32,32]{2,1,0:T(8,128)S(1)} %get-tuple-element.10) | data formatting | bytes 221184
